TPU v7x, 32 devices: a whole 2x2x4 slice. The times are simulated.
32 devices in a mesh: dp: 8 (over z, x), mp: 4 (over y, core).
Axes of the slice: x: 2, y: 2, z: 4, core: 2. Of those that a mesh axis runs over, the one named last changes fastest.
Arguments:
- tokens: float32 [10240, 1024], P(('dp', 'mp')), may hold values from -6 to 6
- cotangent: float32 [10240, 1024], P(('dp', 'mp')), may hold values from -6 to 6
- segments: int32 [10240], P('dp'), may hold values from 0 to 63, as said below
- attention_weights: float32 [2, 4, 1024, 1024], P(None, None, 'dp', 'mp')
- attention_first: float32 [2, 4, 1024, 1024], P(None, None, 'dp', 'mp')
- attention_second: float32 [2, 4, 1024, 1024], P(None, None, 'dp', 'mp')
- dense_weights: float32 [2, 2, 1024, 4096], P(None, None, 'dp', 'mp')
- dense_first: float32 [2, 2, 1024, 4096], P(None, None, 'dp', 'mp')
- dense_second: float32 [2, 2, 1024, 4096], P(None, None, 'dp', 'mp')
- norm_params: float32 [2, 4, 1024], replicated
- norm_first: float32 [2, 4, 1024], replicated
- norm_second: float32 [2, 4, 1024], replicated
Outputs:
- outcome: float32 [10240, 1024], P(('dp', 'mp'))
- grad_tokens: float32 [10240, 1024], P(('dp', 'mp'))
- attention_new: float32 [2, 4, 1024, 1024], P(None, None, 'dp', 'mp')
- attention_first_new: float32 [2, 4, 1024, 1024], P(None, None, 'dp', 'mp')
- attention_second_new: float32 [2, 4, 1024, 1024], P(None, None, 'dp', 'mp')
- attention_copy: bfloat16 [2, 4, 1024, 1024], P(None, None, 'dp', 'mp')
- dense_new: float32 [2, 2, 1024, 4096], P(None, None, 'dp', 'mp')
- dense_first_new: float32 [2, 2, 1024, 4096], P(None, None, 'dp', 'mp')
- dense_second_new: float32 [2, 2, 1024, 4096], P(None, None, 'dp', 'mp')
- dense_copy: bfloat16 [2, 2, 1024, 4096], P(None, None, 'dp', 'mp')
- norm_new: float32 [2, 4, 1024], replicated
- norm_first_new: float32 [2, 4, 1024], replicated
- norm_second_new: float32 [2, 4, 1024], replicated
- norms: float32 [2, 6, 2], replicated
- second_norm_grad: float32 [2, 2, 1024], replicated
Inputs may be any that keep to these rules, and one draw needn't show every extreme that they name: `segments`: in each aligned block of 1280 tokens crop numbers start at 0 and never fall; a block holds 2·8 crops of 50 tokens and 6·8 crops of 10 tokens in an order drawn from the seed.
All inputs are finite; a program needn't handle non-finite values.
Results may differ from a plain program's by a relative error of at most 0.029.
Values may be sent and summed in bfloat16 or wider, within the bound.
No kernel may reach another device: no remote copies, remote signals or barrier semaphores. Data moves between devices by JAX's collectives and lax.ppermute only.
A program may use at most 320 MiB of HBM per device.

v0:
```python
import jax
import jax.numpy as jnp
from jax import lax
from jax.sharding import PartitionSpec as P

D = 1024
HEADS = 16
HD = 64
FF = 4096
STEP = 10
EPS_NORM = 1e-06
BETA_ONE = 0.9
BETA_TWO = 0.999
ADAM_EPS = 1e-06
WEIGHT_DECAY = 0.01
LEARN_RATE = 0.5
MASKED = -1000000000.0


def layer_norm(stream, gain, shift):
    centre = stream - jnp.mean(stream, axis=-1, keepdims=True)
    spread = jnp.mean(centre * centre, axis=-1, keepdims=True)
    return centre * lax.rsqrt(spread + EPS_NORM) * gain + shift


def gelu_exact(values_in):
    return jax.nn.gelu(values_in, approximate=False)


def adam_part(gradient, weight, first, second, decay):
    first_new = BETA_ONE * first + (1.0 - BETA_ONE) * gradient
    second_new = BETA_TWO * second + (1.0 - BETA_TWO) * gradient * gradient
    step_dir = (
        first_new
        / (1.0 - BETA_ONE**STEP)
        / (jnp.sqrt(second_new / (1.0 - BETA_TWO**STEP)) + ADAM_EPS)
        + decay * weight
    )
    return (first_new, second_new, step_dir)


def masked_scores(query, keys_in, same_crop):
    scores = jnp.einsum(
        "qhe,khe->hqk", query, keys_in, preferred_element_type=jnp.float32
    ) * HD ** (-0.5)
    return jnp.where(same_crop, scores, MASKED)


def attend(query, keys_in, values_in, same_crop):
    scores = masked_scores(query, keys_in, same_crop)
    row_max = jnp.max(scores, axis=-1, keepdims=True)
    powered = jnp.exp(scores - row_max)
    row_sum = jnp.sum(powered, axis=-1, keepdims=True)
    shares = (powered / row_sum).astype(jnp.bfloat16)
    attended = jnp.einsum("hqk,khe->qhe", shares, values_in, preferred_element_type=jnp.float32)
    return (attended, row_max + jnp.log(row_sum))


def attend_back(query, keys_in, values_in, same_crop, log_total, grad_attended):
    shares = jnp.exp(masked_scores(query, keys_in, same_crop) - log_total)
    grad_shares = jnp.einsum(
        "qhe,khe->hqk", grad_attended, values_in, preferred_element_type=jnp.float32
    )
    row_inner = jnp.sum(grad_shares * shares, axis=-1, keepdims=True)
    grad_scores = (shares * (grad_shares - row_inner)).astype(jnp.bfloat16)
    score_scale = HD ** (-0.5)
    grad_query = (
        jnp.einsum("hqk,khe->qhe", grad_scores, keys_in, preferred_element_type=jnp.float32)
        * score_scale
    )
    grad_keys = (
        jnp.einsum("hqk,qhe->khe", grad_scores, query, preferred_element_type=jnp.float32)
        * score_scale
    )
    grad_values = jnp.einsum(
        "hqk,qhe->khe",
        shares.astype(jnp.bfloat16),
        grad_attended,
        preferred_element_type=jnp.float32,
    )
    return jnp.stack([grad_query, grad_keys, grad_values], axis=1)


def shards(
    tokens,
    cotangent,
    segments,
    attention_weights,
    attention_first,
    attention_second,
    dense_weights,
    dense_first,
    dense_second,
    norm_params,
    norm_first,
    norm_second,
):
    layers = attention_weights.shape[0]
    token_count = segments.shape[0]
    heads_here = attention_weights.shape[3] // HD
    same_crop = (segments[:, None] == segments[None, :])[None]
    mixer_low = attention_weights.astype(jnp.bfloat16)
    dense_low = dense_weights.astype(jnp.bfloat16)
    copies = []
    for current in range(layers):
        copies.append(
            (
                lax.all_gather(mixer_low[current], "dp", axis=1, tiled=True),
                lax.all_gather(dense_low[current], "dp", axis=1, tiled=True),
            )
        )
    saved_forward = []
    stream = tokens
    for current in range(layers):
        mixer_full, dense_full = copies[current]
        params = norm_params[current]
        normed = layer_norm(stream, params[0], params[1]).astype(jnp.bfloat16)
        gathered = lax.all_gather(normed, "mp", axis=0, tiled=True)
        projected = jnp.einsum(
            "td,sdh->tsh", gathered, mixer_full[:3], preferred_element_type=jnp.float32
        ).astype(jnp.bfloat16)
        split_heads = projected.reshape(token_count, 3, heads_here, HD)
        attended, log_total = attend(
            split_heads[:, 0], split_heads[:, 1], split_heads[:, 2], same_crop
        )
        attended = attended.reshape(token_count, heads_here * HD).astype(jnp.bfloat16)
        middle = stream + lax.psum_scatter(
            jnp.einsum(
                "th,dh->td", attended, mixer_full[3], preferred_element_type=jnp.float32
            ).astype(jnp.bfloat16),
            "mp",
            scatter_dimension=0,
            tiled=True,
        ).astype(jnp.float32)
        normed_two = layer_norm(middle, params[2], params[3]).astype(jnp.bfloat16)
        dense_wide = dense_full
        gathered_two = lax.all_gather(normed_two, "mp", axis=0, tiled=True)
        hidden = jnp.dot(gathered_two, dense_full[0], preferred_element_type=jnp.float32)
        active = gelu_exact(hidden).astype(jnp.bfloat16)
        after_dense = middle + lax.psum_scatter(
            jnp.einsum(
                "tf,df->td", active, dense_full[1], preferred_element_type=jnp.float32
            ).astype(jnp.bfloat16),
            "mp",
            scatter_dimension=0,
            tiled=True,
        ).astype(jnp.float32)
        saved_forward.append(
            (
                stream,
                gathered,
                projected,
                log_total,
                attended,
                middle,
                gathered_two,
                hidden,
                active,
                dense_wide,
            )
        )
        stream = after_dense
    stream_grad = cotangent
    states = [None] * layers
    squares_list = [None] * layers
    vector_list = [None] * layers
    summed_list = [None] * layers
    for current in reversed(range(layers)):
        (
            stream_in,
            gathered,
            projected,
            log_total,
            attended,
            middle,
            gathered_two,
            hidden,
            active,
            dense_wide,
        ) = saved_forward[current]
        mixer_full, dense_full = copies[current]
        params = norm_params[current]
        back_rows = lax.all_gather(stream_grad.astype(jnp.bfloat16), "mp", axis=0, tiled=True)
        grad_active = jnp.dot(back_rows, dense_full[1], preferred_element_type=jnp.float32)
        grad_down = jnp.einsum("td,tf->df", back_rows, active, preferred_element_type=jnp.float32)
        gelu_value, gelu_pull = jax.vjp(gelu_exact, hidden)
        grad_hidden = gelu_pull(grad_active)[0].astype(jnp.bfloat16)
        grad_up = jnp.einsum(
            "td,tf->df", gathered_two, grad_hidden, preferred_element_type=jnp.float32
        )
        grad_normed_two = lax.psum_scatter(
            jnp.einsum(
                "tf,df->td", grad_hidden, dense_full[0], preferred_element_type=jnp.float32
            ).astype(jnp.bfloat16),
            "mp",
            scatter_dimension=0,
            tiled=True,
        ).astype(jnp.float32)
        norm_value, norm_pull = jax.vjp(layer_norm, middle, params[2], params[3])
        grad_middle, grad_gain_two, grad_shift_two = norm_pull(grad_normed_two)
        stream_grad = stream_grad + grad_middle
        back_rows_two = lax.all_gather(stream_grad.astype(jnp.bfloat16), "mp", axis=0, tiled=True)
        grad_attended = jnp.dot(
            back_rows_two, mixer_full[3], preferred_element_type=jnp.float32
        ).astype(jnp.bfloat16)
        grad_output_map = jnp.einsum(
            "td,th->dh", back_rows_two, attended, preferred_element_type=jnp.float32
        )
        split_heads = projected.reshape(token_count, 3, heads_here, HD)
        grad_split = attend_back(
            split_heads[:, 0],
            split_heads[:, 1],
            split_heads[:, 2],
            same_crop,
            log_total,
            grad_attended.reshape(token_count, heads_here, HD),
        )
        grad_projected = grad_split.reshape(token_count, 3, heads_here * HD).astype(jnp.bfloat16)
        grad_inputs_map = jnp.einsum(
            "td,tsh->sdh", gathered, grad_projected, preferred_element_type=jnp.float32
        )
        grad_normed = lax.psum_scatter(
            jnp.einsum(
                "tsh,sdh->td", grad_projected, mixer_full[:3], preferred_element_type=jnp.float32
            ).astype(jnp.bfloat16),
            "mp",
            scatter_dimension=0,
            tiled=True,
        ).astype(jnp.float32)
        norm_value_one, norm_pull_one = jax.vjp(layer_norm, stream_in, params[0], params[1])
        grad_inner, grad_gain_one, grad_shift_one = norm_pull_one(grad_normed)
        stream_grad = stream_grad + grad_inner
        mixer_grad = jnp.concatenate([grad_inputs_map, grad_output_map[None]], axis=0)
        dense_grad = jnp.stack([grad_up, grad_down], axis=0)
        mixer_grad, dense_grad = (
            lax.psum_scatter(mixer_grad, "dp", scatter_dimension=1, tiled=True),
            lax.psum_scatter(dense_grad, "dp", scatter_dimension=1, tiled=True),
        )
        mixer_first, mixer_second, mixer_step = adam_part(
            mixer_grad,
            attention_weights[current],
            attention_first[current],
            attention_second[current],
            WEIGHT_DECAY,
        )
        dense_first_new, dense_second_new, dense_step = adam_part(
            dense_grad,
            dense_weights[current],
            dense_first[current],
            dense_second[current],
            WEIGHT_DECAY,
        )
        weight_squares = jnp.concatenate(
            [
                jnp.sum(attention_weights[current] * attention_weights[current], axis=(1, 2)),
                jnp.sum(dense_weights[current] * dense_weights[current], axis=(1, 2)),
            ]
        )
        step_squares = jnp.concatenate(
            [
                jnp.sum(mixer_step * mixer_step, axis=(1, 2)),
                jnp.sum(dense_step * dense_step, axis=(1, 2)),
            ]
        )
        squares = jnp.stack([weight_squares, step_squares], axis=-1)
        vector_grad = jnp.stack(
            [grad_gain_one, grad_shift_one, grad_gain_two, grad_shift_two], axis=0
        )
        states[current] = (
            mixer_first,
            mixer_second,
            mixer_step,
            dense_first_new,
            dense_second_new,
            dense_step,
        )
        squares_list[current] = squares
        vector_list[current] = vector_grad
        summed_list[current] = lax.psum((squares, vector_grad), ("dp", "mp"))
    total_squares = jnp.stack([entry[0] for entry in summed_list])
    total_vectors = jnp.stack([entry[1] for entry in summed_list])
    sizes_all = jnp.sqrt(total_squares[:, :, 0])
    moves_all = jnp.sqrt(total_squares[:, :, 1])
    trust_all = sizes_all / moves_all
    mixer_new = jnp.stack(
        [
            attention_weights[current]
            - LEARN_RATE * trust_all[current, :4, None, None] * states[current][2]
            for current in range(layers)
        ]
    )
    dense_new = jnp.stack(
        [
            dense_weights[current]
            - LEARN_RATE * trust_all[current, 4:, None, None] * states[current][5]
            for current in range(layers)
        ]
    )
    mixer_first_all = jnp.stack([states[current][0] for current in range(layers)])
    mixer_second_all = jnp.stack([states[current][1] for current in range(layers)])
    dense_first_all = jnp.stack([states[current][3] for current in range(layers)])
    dense_second_all = jnp.stack([states[current][4] for current in range(layers)])
    params_first, params_second, params_step = adam_part(
        total_vectors, norm_params, norm_first, norm_second, 0.0
    )
    params_size = jnp.sqrt(jnp.sum(norm_params * norm_params, axis=-1))
    params_move = jnp.sqrt(jnp.sum(params_step * params_step, axis=-1))
    params_new = norm_params - LEARN_RATE * (params_size / params_move)[:, :, None] * params_step
    mixer_entries = float(D * HEADS * HD) ** 0.5
    dense_entries = float(D * FF) ** 0.5
    entry_roots = jnp.array([mixer_entries] * 4 + [dense_entries] * 2, jnp.float32)
    norms = jnp.stack([sizes_all / entry_roots[None, :], moves_all / entry_roots[None, :]], axis=-1)
    second_norm_grad = total_vectors[:, 2:4]
    return (
        stream,
        stream_grad,
        mixer_new,
        mixer_first_all,
        mixer_second_all,
        mixer_new.astype(jnp.bfloat16),
        dense_new,
        dense_first_all,
        dense_second_all,
        dense_new.astype(jnp.bfloat16),
        params_new,
        params_first,
        params_second,
        norms,
        second_norm_grad,
    )


def solution(mesh):
    in_specs = (
        P(("dp", "mp"), None),
        P(("dp", "mp"), None),
        P("dp"),
        P(None, None, "dp", "mp"),
        P(None, None, "dp", "mp"),
        P(None, None, "dp", "mp"),
        P(None, None, "dp", "mp"),
        P(None, None, "dp", "mp"),
        P(None, None, "dp", "mp"),
        P(),
        P(),
        P(),
    )
    out_specs = (
        P(("dp", "mp"), None),
        P(("dp", "mp"), None),
        P(None, None, "dp", "mp"),
        P(None, None, "dp", "mp"),
        P(None, None, "dp", "mp"),
        P(None, None, "dp", "mp"),
        P(None, None, "dp", "mp"),
        P(None, None, "dp", "mp"),
        P(None, None, "dp", "mp"),
        P(None, None, "dp", "mp"),
        P(),
        P(),
        P(),
        P(),
        P(),
    )
    return jax.shard_map(shards, mesh=mesh, in_specs=in_specs, out_specs=out_specs, check_vma=False)
```

profile of v0, /device:TPU:0, one launch (start us, length us, event | category | flops | bytes accessed | tf_op | source)
XLA Modules:
  0.0 1625.0 jit_solution(6079072630626825102)
XLA Ops:
  13.5 51.0 %all-gather.33.cloned.1.call-done = bf16[1,4,1024,256]{2,3,1,0:T(8,128)(2,1)} async-done(((bf16[1,4,128,256]{2,3,1,0:T(8,128)(2,1)}), bf16[1,4,1024,256]{2,3,1,0:T(8,128)(2,1)}) %all-gather.33.cloned.1.call-update) | async-done | bytes 2097168 | tf_op jit(solution)/shard_map/all_gather | solution.py:108
  64.4 25.9 %all-gather.17.cloned.1.call-done = bf16[1280,1024]{1,0:T(8,128)(2,1)} async-done(((bf16[320,1024]{1,0:T(8,128)(2,1)}), bf16[1280,1024]{1,0:T(8,128)(2,1)}) %all-gather.17.cloned.1.call-update) | async-done | bytes 2621456 | tf_op jit(solution)/shard_map/all_gather | solution.py:118
  94.8 11.0 fusion.121
  105.9 10.6 fusion.2
  116.5 11.0 fusion.43
  133.2 33.5 %reduce-scatter.13.cloned.1.call-done = bf16[320,1024]{1,0:T(8,128)(2,1)} async-done(((bf16[1280,1024]{1,0:T(8,128)(2,1)}), bf16[320,1024]{1,0:T(8,128)(2,1)}) %reduce-scatter.13.cloned.1.call-update) | async-done | bytes 655376 | tf_op jit(solution)/shard_map/reduce_scatter | solution.py:127
  169.5 10.4 reduce-scatter.15.cloned.1.call-start
  179.9 63.0 %all-gather.35.cloned.1.call-done = bf16[1,2,1024,1024]{3,2,1,0:T(8,128)(2,1)} async-done(((bf16[1,2,128,1024]{3,2,1,0:T(8,128)(2,1)}), bf16[1,2,1024,1024]{3,2,1,0:T(8,128)(2,1)}) %all-gather.35.cloned.1.call-update) | async-done | bytes 4194320 | tf_op jit(solution)/shard_map/all_gather | solution.py:109
  243.0 25.9 %all-gather.19.cloned.1.call-done = bf16[1280,1024]{1,0:T(8,128)(2,1)} async-done(((bf16[320,1024]{1,0:T(8,128)(2,1)}), bf16[1280,1024]{1,0:T(8,128)(2,1)}) %all-gather.19.cloned.1.call-update) | async-done | bytes 2621456 | tf_op jit(solution)/shard_map/all_gather | solution.py:137
  268.9 17.2 %multiply_convert_fusion.3 = (bf16[1280,1024]{1,0:T(8,128)(2,1)S(1)}, f32[1280,1024]{1,0:T(8,128)}, f32[1280,1024]{1,0:T(8,128)}) fusion(bf16[1280,1024]{1,0:T(8,128)(2,1)} %all-gather.19.cloned.1.call-done, bf16[1,2,1024,1024]{3,2,1,0:T(8,128)(2,1)} %all-gather.35.cloned.1.call-done), kind=kOutput, calls=%fused_computation.47 | convolution fusion | flops 2769551360 | bytes 17825792 | tf_op jit(solution)/shard_map/dot_general | solution.py:138
  292.7 34.0 %reduce-scatter.15.cloned.1.call-done = bf16[320,1024]{1,0:T(8,128)(2,1)} async-done(((bf16[1280,1024]{1,0:T(8,128)(2,1)}), bf16[320,1024]{1,0:T(8,128)(2,1)}) %reduce-scatter.15.cloned.1.call-update) | async-done | bytes 655376 | tf_op jit(solution)/shard_map/reduce_scatter | solution.py:140
  329.6 50.9 %all-gather.37.cloned.1.call-done = bf16[1,4,1024,256]{2,3,1,0:T(8,128)(2,1)} async-done(((bf16[1,4,128,256]{2,3,1,0:T(8,128)(2,1)}), bf16[1,4,1024,256]{2,3,1,0:T(8,128)(2,1)}) %all-gather.37.cloned.1.call-update) | async-done | bytes 2097168 | tf_op jit(solution)/shard_map/all_gather | solution.py:108
  380.4 25.9 %all-gather.21.cloned.1.call-done = bf16[1280,1024]{1,0:T(8,128)(2,1)} async-done(((bf16[320,1024]{1,0:T(8,128)(2,1)}), bf16[1280,1024]{1,0:T(8,128)(2,1)}) %all-gather.21.cloned.1.call-update) | async-done | bytes 2621456 | tf_op jit(solution)/shard_map/all_gather | solution.py:118
  410.8 11.0 fusion.122
  421.8 10.6 fusion.3
  432.4 11.0 fusion.42
  448.3 34.2 %reduce-scatter.17.cloned.1.call-done = bf16[320,1024]{1,0:T(8,128)(2,1)} async-done(((bf16[1280,1024]{1,0:T(8,128)(2,1)}), bf16[320,1024]{1,0:T(8,128)(2,1)}) %reduce-scatter.17.cloned.1.call-update) | async-done | bytes 655376 | tf_op jit(solution)/shard_map/reduce_scatter | solution.py:127
  488.1 70.7 %all-gather.39.cloned.1.call-done = bf16[1,2,1024,1024]{3,2,1,0:T(8,128)(2,1)} async-done(((bf16[1,2,128,1024]{3,2,1,0:T(8,128)(2,1)}), bf16[1,2,1024,1024]{3,2,1,0:T(8,128)(2,1)}) %all-gather.39.cloned.1.call-update) | async-done | bytes 4194320 | tf_op jit(solution)/shard_map/all_gather | solution.py:109
  558.8 26.1 %all-gather.23.cloned.1.call-done = bf16[1280,1024]{1,0:T(8,128)(2,1)} async-done(((bf16[320,1024]{1,0:T(8,128)(2,1)}), bf16[1280,1024]{1,0:T(8,128)(2,1)}) %all-gather.23.cloned.1.call-update) | async-done | bytes 2621456 | tf_op jit(solution)/shard_map/all_gather | solution.py:137
  584.9 17.3 %multiply_convert_fusion.2 = (bf16[1280,1024]{1,0:T(8,128)(2,1)}, f32[1280,1024]{1,0:T(8,128)}, f32[1280,1024]{1,0:T(8,128)}) fusion(bf16[1280,1024]{1,0:T(8,128)(2,1)} %all-gather.23.cloned.1.call-done, bf16[1,2,1024,1024]{3,2,1,0:T(8,128)(2,1)} %all-gather.39.cloned.1.call-done), kind=kOutput, calls=%fused_computation.34 | convolution fusion | flops 2769551360 | bytes 17825792 | tf_op jit(solution)/shard_map/dot_general | solution.py:138
  602.2 10.3 all-gather.25.cloned.1.call-done
  612.5 9.8 add_convert_fusion.1
  628.2 6.8 convolution_convert_fusion.4
  635.0 27.9 %reduce-scatter.21.cloned.1.call-done = bf16[320,1024]{1,0:T(8,128)(2,1)} async-done(((bf16[1280,1024]{1,0:T(8,128)(2,1)}), bf16[320,1024]{1,0:T(8,128)(2,1)}) %reduce-scatter.21.cloned.1.call-update) | async-done | bytes 655376 | tf_op jit(solution)/shard_map/reduce_scatter | solution.py:191
  665.2 34.9 %reduce-scatter.19.cloned.1.call-done = bf16[320,1024]{1,0:T(8,128)(2,1)} async-done(((bf16[1280,1024]{1,0:T(8,128)(2,1)}), bf16[320,1024]{1,0:T(8,128)(2,1)}) %reduce-scatter.19.cloned.1.call-update) | async-done | bytes 655376 | tf_op jit(solution)/shard_map/reduce_scatter | solution.py:140
  705.4 25.5 %all-gather.27.cloned.1.call-done = bf16[1280,1024]{1,0:T(8,128)(2,1)} async-done(((bf16[320,1024]{1,0:T(8,128)(2,1)}), bf16[1280,1024]{1,0:T(8,128)(2,1)}) %all-gather.27.cloned.1.call-update) | async-done | bytes 2621456 | tf_op jit(solution)/shard_map/all_gather | solution.py:202
  733.5 10.8 fusion.32
  744.3 16.7 %multiply_reduce_fusion.1 = (f32[4,1280]{1,0:T(4,128)S(1)}, f32[4,1280,1280]{1,2,0:T(8,128)}) fusion(f32[4,1280,1280]{1,2,0:T(8,128)} %get-tuple-element.129, f32[4,1280]{1,0:T(4,128)S(1)} %log_add_fusion.1, bf16[1280,4,64]{0,2,1:T(8,128)(2,1)S(1)} %bitcast.336, bf16[1280,3,4,64]{0,3,2,1:T(8,128)(2,1)} %bitcast.346), kind=kOutput, calls=%fused_computation.8 | convolution fusion | flops 858516480 | bytes 53780480 | tf_op jit(solution)/shard_map/qhe,khe->hqk/dot_general | solution.py:61
  761.0 22.2 %multiply_convert_fusion.1 = bf16[4,1280,1280]{1,2,0:T(8,128)(2,1)} fusion(f32[4,1280,1280]{1,2,0:T(8,128)} %get-tuple-element.132, f32[4,1280,1280]{1,2,0:T(8,128)} %get-tuple-element.129, f32[4,1280]{1,0:T(4,128)S(1)} %get-tuple-element.131, f32[4,1280]{1,0:T(4,128)S(1)} %log_add_fusion.1), kind=kLoop, calls=%fused_computation.7 | loop fusion | flops 26214400 | bytes 65576960 | tf_op jit(solution)/shard_map/convert_element_type | solution.py:65
  783.3 8.8 fusion.39
  792.1 7.1 fusion.38
  807.4 34.5 %reduce-scatter.23.cloned.1.call-done = bf16[320,1024]{1,0:T(8,128)(2,1)} async-done(((bf16[1280,1024]{1,0:T(8,128)(2,1)}), bf16[320,1024]{1,0:T(8,128)(2,1)}) %reduce-scatter.23.cloned.1.call-update) | async-done | bytes 655376 | tf_op jit(solution)/shard_map/reduce_scatter | solution.py:222
  847.4 25.7 %all-gather.29.cloned.1.call-done = bf16[1280,1024]{1,0:T(8,128)(2,1)} async-done(((bf16[320,1024]{1,0:T(8,128)(2,1)}), bf16[1280,1024]{1,0:T(8,128)(2,1)}) %all-gather.29.cloned.1.call-update) | async-done | bytes 2621456 | tf_op jit(solution)/shard_map/all_gather | solution.py:183
  873.0 9.8 add_convert_fusion
  888.7 34.8 %reduce-scatter.25.cloned.1.call-done = bf16[320,1024]{1,0:T(8,128)(2,1)} async-done(((bf16[1280,1024]{1,0:T(8,128)(2,1)}), bf16[320,1024]{1,0:T(8,128)(2,1)}) %reduce-scatter.25.cloned.1.call-update) | async-done | bytes 655376 | tf_op jit(solution)/shard_map/reduce_scatter | solution.py:191
  929.5 25.2 %all-gather.31.cloned.1.call-done = bf16[1280,1024]{1,0:T(8,128)(2,1)} async-done(((bf16[320,1024]{1,0:T(8,128)(2,1)}), bf16[1280,1024]{1,0:T(8,128)(2,1)}) %all-gather.31.cloned.1.call-update) | async-done | bytes 2621456 | tf_op jit(solution)/shard_map/all_gather | solution.py:202
  957.4 11.7 fusion.35
  969.1 16.6 %multiply_reduce_fusion = (f32[4,1280]{1,0:T(4,128)S(1)}, f32[4,1280,1280]{1,2,0:T(8,128)}) fusion(f32[4,1280,1280]{1,2,0:T(8,128)} %get-tuple-element.126, f32[4,1280]{1,0:T(4,128)S(1)} %log_add_fusion, bf16[1280,4,64]{0,2,1:T(8,128)(2,1)S(1)} %bitcast.338, bf16[1280,3,4,64]{0,3,2,1:T(8,128)(2,1)S(1)} %bitcast.341), kind=kOutput, calls=%fused_computation.5 | convolution fusion | flops 858516480 | bytes 53780480 | tf_op jit(solution)/shard_map/qhe,khe->hqk/dot_general | solution.py:61
  985.7 22.1 %multiply_convert_fusion = bf16[4,1280,1280]{1,2,0:T(8,128)(2,1)} fusion(f32[4,1280,1280]{1,2,0:T(8,128)} %get-tuple-element.134, f32[4,1280,1280]{1,2,0:T(8,128)} %get-tuple-element.126, f32[4,1280]{1,0:T(4,128)S(1)} %get-tuple-element.133, f32[4,1280]{1,0:T(4,128)S(1)} %log_add_fusion), kind=kLoop, calls=%fused_computation.4 | loop fusion | flops 26214400 | bytes 65576960 | tf_op jit(solution)/shard_map/convert_element_type | solution.py:65
  1007.8 8.8 fusion.41
  1016.5 7.1 fusion.40
  1030.9 5.8 convolution_bitcast_fusion
  1044.0 5.7 convolution_bitcast_fusion.3
  1086.9 131.2 %reduce-scatter.35.cloned.1.call-done = f32[2,128,1024]{2,1,0:T(8,128)} async-done(((f32[2,1024,1024]{2,1,0:T(8,128)}), f32[2,128,1024]{2,1,0:T(8,128)}) %reduce-scatter.35.cloned.1.call-update) | async-done | bytes 1048592 | tf_op jit(solution)/shard_map/reduce_scatter | solution.py:237
  1218.2 152.1 %reduce-scatter.31.cloned.1.call-done = f32[2,128,1024]{2,1,0:T(8,128)} async-done(((f32[2,1024,1024]{2,1,0:T(8,128)}), f32[2,128,1024]{2,1,0:T(8,128)}) %reduce-scatter.31.cloned.1.call-update) | async-done | bytes 1048592 | tf_op jit(solution)/shard_map/reduce_scatter | solution.py:237
  1378.2 83.1 %reduce-scatter.33.cloned.1.call-done = f32[4,128,256]{1,2,0:T(8,128)} async-done(((f32[4,1024,256]{1,2,0:T(8,128)}), f32[4,128,256]{1,2,0:T(8,128)}) %reduce-scatter.33.cloned.1.call-update) | async-done | bytes 524304 | tf_op jit(solution)/shard_map/reduce_scatter | solution.py:236
  1461.4 92.2 %reduce-scatter.29.cloned.1.call-done = f32[4,128,256]{1,2,0:T(8,128)} async-done(((f32[4,1024,256]{1,2,0:T(8,128)}), f32[4,128,256]{1,2,0:T(8,128)}) %reduce-scatter.29.cloned.1.call-update) | async-done | bytes 524304 | tf_op jit(solution)/shard_map/reduce_scatter | solution.py:236
  1558.0 40.8 %all-reduce = (f32[1,6,2]{1,2,0:T(2,128)S(1)}, f32[1,6,2]{1,2,0:T(2,128)S(1)}, f32[1,4,1024]{2,1,0:T(4,128)S(1)}, f32[1,4,1024]{2,1,0:T(4,128)S(1)}) all-reduce(f32[1,6,2]{1,2,0:T(2,128)S(1)} %maximum_bitcast_fusion.2, f32[1,6,2]{1,2,0:T(2,128)S(1)} %maximum_bitcast_fusion.3, ...), channel_id=1, replica_groups=mesh['dp'=8,'mp'=4] {'dp','mp'}, use_global_device_ids=true, to_apply=%region_36.37 | all-reduce | flops 8216 | bytes 65728 | tf_op jit(solution)/shard_map/psum | solution.py:279
  (327 shorter events, 170.0 us)
Async XLA Ops:
  7.2 57.3 %all-gather.33.cloned.1.call-start = ((), (), s32[]{:S(2)}) async-start(), calls=%async_computation.32 | async-start | bytes 2359296 | tf_op jit(solution)/shard_map/all_gather | solution.py:108
  10.0 80.3 %all-gather.17.cloned.1.call-start = ((), (), s32[]{:S(2)}) async-start(), calls=%async_computation.12 | async-start | bytes 3276800 | tf_op jit(solution)/shard_map/all_gather | solution.py:118
  10.6 84.2 %copy-start.58 = (f32[320]{0:T(512)}, f32[320]{0:T(512)S(1)}, u32[]{:S(2)}) copy-start(f32[320]{0:T(512)S(1)} %fusion.93) | copy-start | bytes 3844
  11.2 157.1 %copy-start.48 = (f32[1,1,1024]{2,1,0:T(1,128)}, f32[1,1,1024]{2,1,0:T(1,128)S(1)}, u32[]{:S(2)}) copy-start(f32[1,1,1024]{2,1,0:T(1,128)S(1)} %get-tuple-element.115) | copy-start | bytes 12292
  11.2 317.2 %copy-start.38 = (f32[1,1,1024]{2,1,0:T(1,128)}, f32[1,1,1024]{2,1,0:T(1,128)S(1)}, u32[]{:S(2)}) copy-start(f32[1,1,1024]{2,1,0:T(1,128)S(1)} %get-tuple-element.113) | copy-start | bytes 12292
  12.4 154.3 %reduce-scatter.13.cloned.1.call-start = ((), (), s32[]{:S(2)}) async-start(), calls=%async_computation.13 | async-start | bytes 3276800 | tf_op jit(solution)/shard_map/reduce_scatter | solution.py:127
  13.4 81.4 %copy-start.20 = (pred[1280,1280]{0,1:T(8,128)(4,1)}, pred[1280,1280]{0,1:T(8,128)(4,1)S(1)}, u32[]{:S(2)}) copy-start(pred[1280,1280]{0,1:T(8,128)(4,1)S(1)} %broadcast_compare_fusion) | copy-start | bytes 4915204
  131.9 111.1 %all-gather.35.cloned.1.call-start = ((), (), s32[]{:S(2)}) async-start(), calls=%async_computation.33 | async-start | bytes 4718592 | tf_op jit(solution)/shard_map/all_gather | solution.py:109
  133.2 135.7 %all-gather.19.cloned.1.call-start = ((), (), s32[]{:S(2)}) async-start(), calls=%async_computation.14 | async-start | bytes 3276800 | tf_op jit(solution)/shard_map/all_gather | solution.py:137
  168.0 158.7 %copy-start.2 = (f32[320,1024]{1,0:T(8,128)}, f32[320,1024]{1,0:T(8,128)S(1)}, u32[]{:S(2)}) copy-start(f32[320,1024]{1,0:T(8,128)S(1)} %get-tuple-element.79) | copy-start | bytes 3932164
  168.0 118.1 %copy-start.51 = (f32[320]{0:T(512)}, f32[320]{0:T(512)S(1)}, u32[]{:S(2)}) copy-start(f32[320]{0:T(512)S(1)} %broadcast_multiply_fusion.2) | copy-start | bytes 3844
  168.3 117.8 %copy-start.64 = (f32[320]{0:T(512)}, f32[320]{0:T(512)S(1)}, u32[]{:S(2)}) copy-start(f32[320]{0:T(512)S(1)} %multiply_reduce_fusion.4) | copy-start | bytes 3844
  168.4 117.8 %copy-start.56 = (f32[320]{0:T(512)}, f32[320]{0:T(512)S(1)}, u32[]{:S(2)}) copy-start(f32[320]{0:T(512)S(1)} %fusion.94) | copy-start | bytes 3844
  169.5 157.2 %reduce-scatter.15.cloned.1.call-start = ((), (), s32[]{:S(2)}) async-start(), calls=%async_computation.15 | async-start | bytes 3276800 | tf_op jit(solution)/shard_map/reduce_scatter | solution.py:140
  291.9 88.6 %all-gather.37.cloned.1.call-start = ((), (), s32[]{:S(2)}) async-start(), calls=%async_computation.34 | async-start | bytes 2359296 | tf_op jit(solution)/shard_map/all_gather | solution.py:108
  292.6 113.7 %all-gather.21.cloned.1.call-start = ((), (), s32[]{:S(2)}) async-start(), calls=%async_computation.16 | async-start | bytes 3276800 | tf_op jit(solution)/shard_map/all_gather | solution.py:118
  329.5 81.3 %copy-start.21 = (pred[1280,1280]{0,1:T(8,128)(4,1)S(1)}, pred[1280,1280]{0,1:T(8,128)(4,1)}, u32[]{:S(2)}) copy-start(pred[1280,1280]{0,1:T(8,128)(4,1)} %copy-done.20) | copy-start | bytes 4915204
  329.5 153.0 %reduce-scatter.17.cloned.1.call-start = ((), (), s32[]{:S(2)}) async-start(), calls=%async_computation.17 | async-start | bytes 3276800 | tf_op jit(solution)/shard_map/reduce_scatter | solution.py:127
  447.7 36.5 %copy-start.50 = (f32[1,1,1024]{2,1,0:T(1,128)S(1)}, f32[1,1,1024]{2,1,0:T(1,128)}, u32[]{:S(2)}) copy-start(f32[1,1,1024]{2,1,0:T(1,128)} %get-tuple-element.110) | copy-start | bytes 12292
  447.7 36.5 %copy-start.70 = (f32[1,1,1024]{2,1,0:T(1,128)S(1)}, f32[1,1,1024]{2,1,0:T(1,128)}, u32[]{:S(2)}) copy-start(f32[1,1,1024]{2,1,0:T(1,128)} %get-tuple-element.111) | copy-start | bytes 12292
  447.7 111.1 %all-gather.39.cloned.1.call-start = ((), (), s32[]{:S(2)}) async-start(), calls=%async_computation.35 | async-start | bytes 4718592 | tf_op jit(solution)/shard_map/all_gather | solution.py:109
  448.3 136.6 %all-gather.23.cloned.1.call-start = ((), (), s32[]{:S(2)}) async-start(), calls=%async_computation.18 | async-start | bytes 3276800 | tf_op jit(solution)/shard_map/all_gather | solution.py:137
  485.3 127.2 %all-gather.25.cloned.1.call-start = ((), (), s32[]{:S(2)}) async-start(), calls=%async_computation.20 | async-start | bytes 3276800 | tf_op jit(solution)/shard_map/all_gather | solution.py:183
  487.6 175.3 %reduce-scatter.21.cloned.1.call-start = ((), (), s32[]{:S(2)}) async-start(), calls=%async_computation.21 | async-start | bytes 3276800 | tf_op jit(solution)/shard_map/reduce_scatter | solution.py:191
  628.1 71.9 %reduce-scatter.19.cloned.1.call-start = ((), (), s32[]{:S(2)}) async-start(), calls=%async_computation.19 | async-start | bytes 3276800 | tf_op jit(solution)/shard_map/reduce_scatter | solution.py:140
  635.0 95.9 %all-gather.27.cloned.1.call-start = ((), (), s32[]{:S(2)}) async-start(), calls=%async_computation.22 | async-start | bytes 3276800 | tf_op jit(solution)/shard_map/all_gather | solution.py:202
  705.1 136.9 %reduce-scatter.23.cloned.1.call-start = ((), (), s32[]{:S(2)}) async-start(), calls=%async_computation.23 | async-start | bytes 3276800 | tf_op jit(solution)/shard_map/reduce_scatter | solution.py:222
  807.1 34.9 %copy-start.47 = (f32[320]{0:T(512)S(1)}, f32[320]{0:T(512)}, u32[]{:S(2)}) copy-start(f32[320]{0:T(512)} %copy-done.46) | copy-start | bytes 3844
  807.1 36.4 %copy-start.67 = (f32[320]{0:T(512)S(1)}, f32[320]{0:T(512)}, u32[]{:S(2)}) copy-start(f32[320]{0:T(512)} %copy-done.66) | copy-start | bytes 3844
  807.1 36.5 %copy-start.61 = (f32[320]{0:T(512)S(1)}, f32[320]{0:T(512)}, u32[]{:S(2)}) copy-start(f32[320]{0:T(512)} %copy-done.60) | copy-start | bytes 3844
  807.2 38.2 %copy-start.10 = (f32[320,1024]{1,0:T(8,128)S(1)}, f32[320,1024]{1,0:T(8,128)}, u32[]{:S(2)}) copy-start(f32[320,1024]{1,0:T(8,128)} %param.14) | copy-start | bytes 3932164
  807.2 65.8 %all-gather.29.cloned.1.call-start = ((), (), s32[]{:S(2)}) async-start(), calls=%async_computation.24 | async-start | bytes 3276800 | tf_op jit(solution)/shard_map/all_gather | solution.py:183
  847.3 76.2 %reduce-scatter.25.cloned.1.call-start = ((), (), s32[]{:S(2)}) async-start(), calls=%async_computation.25 | async-start | bytes 3276800 | tf_op jit(solution)/shard_map/reduce_scatter | solution.py:191
  888.6 34.9 %copy-start.3 = (f32[320,1024]{1,0:T(8,128)S(1)}, f32[320,1024]{1,0:T(8,128)}, u32[]{:S(2)}) copy-start(f32[320,1024]{1,0:T(8,128)} %copy-done.2) | copy-start | bytes 3932164
  888.6 34.9 %copy-start.49 = (f32[1,1,1024]{2,1,0:T(1,128)S(1)}, f32[1,1,1024]{2,1,0:T(1,128)}, u32[]{:S(2)}) copy-start(f32[1,1,1024]{2,1,0:T(1,128)} %copy-done.48) | copy-start | bytes 12292
  888.6 34.9 %copy-start.52 = (f32[320]{0:T(512)S(1)}, f32[320]{0:T(512)}, u32[]{:S(2)}) copy-start(f32[320]{0:T(512)} %copy-done.51) | copy-start | bytes 3844
  888.6 34.9 %copy-start.57 = (f32[320]{0:T(512)S(1)}, f32[320]{0:T(512)}, u32[]{:S(2)}) copy-start(f32[320]{0:T(512)} %copy-done.56) | copy-start | bytes 3844
  888.6 36.5 %copy-start.65 = (f32[320]{0:T(512)S(1)}, f32[320]{0:T(512)}, u32[]{:S(2)}) copy-start(f32[320]{0:T(512)} %copy-done.64) | copy-start | bytes 3844
  888.7 39.1 %copy-start.11 = (f32[320,1024]{1,0:T(8,128)S(1)}, f32[320,1024]{1,0:T(8,128)}, u32[]{:S(2)}) copy-start(f32[320,1024]{1,0:T(8,128)} %get-tuple-element.67) | copy-start | bytes 3932164
  888.7 66.0 %all-gather.31.cloned.1.call-start = ((), (), s32[]{:S(2)}) async-start(), calls=%async_computation.26 | async-start | bytes 3276800 | tf_op jit(solution)/shard_map/all_gather | solution.py:202
  929.0 151.0 %reduce-scatter.27.cloned.1.call-start = ((), (), s32[]{:S(2)}) async-start(), calls=%async_computation.27 | async-start | bytes 3276800 | tf_op jit(solution)/shard_map/reduce_scatter | solution.py:222
  1030.6 187.5 %reduce-scatter.35.cloned.1.call-start = ((), (), s32[]{:S(2)}) async-start(), calls=%async_computation.31 | async-start | bytes 9437184 | tf_op jit(solution)/shard_map/reduce_scatter | solution.py:237
  1043.7 326.5 %reduce-scatter.31.cloned.1.call-start = ((), (), s32[]{:S(2)}) async-start(), calls=%async_computation.29 | async-start | bytes 9437184 | tf_op jit(solution)/shard_map/reduce_scatter | solution.py:237
  1056.9 404.5 %reduce-scatter.33.cloned.1.call-start = ((), (), s32[]{:S(2)}) async-start(), calls=%async_computation.30 | async-start | bytes 4718592 | tf_op jit(solution)/shard_map/reduce_scatter | solution.py:236
  1066.2 487.4 %reduce-scatter.29.cloned.1.call-start = ((), (), s32[]{:S(2)}) async-start(), calls=%async_computation.28 | async-start | bytes 4718592 | tf_op jit(solution)/shard_map/reduce_scatter | solution.py:236
  1083.4 286.8 %copy-start.5 = (f32[2,2,128,1024]{3,2,1,0:T(8,128)S(1)}, f32[2,2,128,1024]{3,2,1,0:T(8,128)}, u32[]{:S(2)}) copy-start(f32[2,2,128,1024]{3,2,1,0:T(8,128)} %param.19) | copy-start | bytes 6291460
  1375.9 177.6 %copy-start.7 = (f32[2,4,128,256]{2,3,1,0:T(8,128)S(1)}, f32[2,4,128,256]{2,3,1,0:T(8,128)}, u32[]{:S(2)}) copy-start(f32[2,4,128,256]{2,3,1,0:T(8,128)} %copy-done.6) | copy-start | bytes 3145732
  1378.2 220.5 %copy-start.71 = (f32[6]{0:T(128)S(1)}, f32[6]{0:T(128)}, u32[]{:S(2)}) copy-start(f32[6]{0:T(128)} %constant.139) | copy-start | bytes 76
  (59 other events, 317.7 us)
Sparse Core Ops, SparseCore 0:
  10.6 53.7 all-gather.32
  66.6 23.7 all-gather.16
  132.0 34.6 reduce-scatter.12
  169.6 73.3 all-gather.34
  245.0 23.8 all-gather.18
  292.0 34.6 reduce-scatter.14
  329.3 51.0 all-gather.36
  382.6 23.7 all-gather.20
  447.8 34.6 reduce-scatter.16
  485.4 73.3 all-gather.38
  561.0 23.8 all-gather.22
  586.9 25.5 all-gather.24
  628.3 34.6 reduce-scatter.20
  665.3 34.6 reduce-scatter.18
  705.2 25.5 all-gather.26
  807.3 34.6 reduce-scatter.22
  847.4 25.5 all-gather.28
  888.8 34.6 reduce-scatter.24
  929.1 25.5 all-gather.30
  1030.7 34.6 reduce-scatter.26
  1069.1 149.0 reduce-scatter.34
  1222.2 147.9 reduce-scatter.30
  1373.9 87.4 reduce-scatter.32
  1465.3 88.2 reduce-scatter.28
where the time goes:
time: 1630 us; the launch traced here: 1620 us
  waiting for transfers between devices  1120 us (69%)
  matrix products  266 us (16%)
  other arithmetic  138 us (8%)
  blocking collectives  40.8 us (3%)
  local copies, waits for them, and re-layouts  31 us (2%)
    reduce_scatter x2, waiting for transfers between devices, shards(): lax.psum_scatter(dense_grad, 'dp', scatter_dimension=1, tiled=True)  283 us
    reduce_scatter x2, waiting for transfers between devices, shards(): lax.psum_scatter(mixer_grad, 'dp', scatter_dimension=1, tiled=True)  175 us
    all_gather x2, waiting for transfers between devices, shards(): lax.all_gather(dense_low[current], 'dp', axis=1, tiled=True)  134 us
    all_gather x2, waiting for transfers between devices, shards(): lax.all_gather(mixer_low[current], 'dp', axis=1, tiled=True)  102 us
    all_gather x4, waiting for transfers between devices, shards(): lax.all_gather(stream_grad.astype(jnp.bfloat16), 'mp', axis=0, tiled=True)  86.7 us
    reduce_scatter x2, waiting for transfers between devices, shards(): lax.psum_scatter(jnp.einsum('tf,df->td', active, dense_full[1], preferred...  68.9 us
    reduce_scatter x2, waiting for transfers between devices, shards(): lax.psum_scatter(jnp.einsum('th,dh->td', attended, mixer_full[3], preferr...  67.7 us
    reduce_scatter x2, waiting for transfers between devices, shards(): lax.psum_scatter(jnp.einsum('tf,df->td', grad_hidden, dense_full[0], pref...  62.7 us
  transfers between devices with their start and end apart: 24, of which 23 were waited for; matrix products, arithmetic and copies ran while one was open for 6% of the time, Pallas kernels for 0%

commit v1 on v0

--- a/solution.py
+++ b/solution.py
@@ -134,7 +134,14 @@
         ).astype(jnp.float32)
         normed_two = layer_norm(middle, params[2], params[3]).astype(jnp.bfloat16)
         dense_wide = dense_full
-        gathered_two = lax.all_gather(normed_two, "mp", axis=0, tiled=True)
+        ring = [normed_two]
+        for hop in range(3):
+            ring.append(lax.ppermute(ring[-1], "mp", [(dev, (dev + 1) % 4) for dev in range(4)]))
+        gathered_two = jnp.roll(
+            jnp.concatenate(ring[::-1], axis=0),
+            (lax.axis_index("mp") + 1) * ring[0].shape[0],
+            axis=0,
+        )
         hidden = jnp.dot(gathered_two, dense_full[0], preferred_element_type=jnp.float32)
         active = gelu_exact(hidden).astype(jnp.bfloat16)
         after_dense = middle + lax.psum_scatter(

time: 1630 us -> 1580 us (0.969)
  waiting for transfers between devices: 1120 us -> 1040 us
  other arithmetic: 138 us -> 166 us
    all_gather x2, waiting for transfers between devices: 134 us -> 56.1 us  [shards(): lax.all_gather(dense_low[current], 'dp', axis=1, tiled=True)]
    ppermute x0 -> x6, waiting for transfers between devices: none -> 58.2 us  [shards(): lax.ppermute(ring[-1], 'mp', [(dev, (dev + 1) % 4) for dev in range(4)])]
    all_gather x2 -> x0, waiting for transfers between devices: 52 us -> none  [shards(): gathered_two = lax.all_gather(normed_two, 'mp', axis=0, tiled=True)]
    concatenate x0 -> x2, other arithmetic: none -> 30 us  [shards(): jnp.roll(jnp.concatenate(ring[::-1], axis=0), (lax.axis_index('mp') + 1)...]
  transfers between devices with their start and end apart: 24 -> 28, of which waited for: 23 -> 27; matrix products, arithmetic and copies ran while one was open for 6% -> 8% of each run, Pallas kernels for 0% -> 0%
where the time goes in v1:
time: 1580 us; the launch traced here: 1570 us
  waiting for transfers between devices  1040 us (66%)
  matrix products  265 us (17%)
  other arithmetic  166 us (11%)
  blocking collectives  40.8 us (3%)
  local copies, waits for them, and re-layouts  37 us (2%)
  between operations  16 us (1%)
    reduce_scatter x2, waiting for transfers between devices, shards(): lax.psum_scatter(dense_grad, 'dp', scatter_dimension=1, tiled=True)  281 us
    reduce_scatter x2, waiting for transfers between devices, shards(): lax.psum_scatter(mixer_grad, 'dp', scatter_dimension=1, tiled=True)  175 us
    all_gather x2, waiting for transfers between devices, shards(): lax.all_gather(mixer_low[current], 'dp', axis=1, tiled=True)  102 us
    all_gather x4, waiting for transfers between devices, shards(): lax.all_gather(stream_grad.astype(jnp.bfloat16), 'mp', axis=0, tiled=True)  84.8 us
    reduce_scatter x2, waiting for transfers between devices, shards(): lax.psum_scatter(jnp.einsum('th,dh->td', attended, mixer_full[3], preferr...  67.5 us
    reduce_scatter x2, waiting for transfers between devices, shards(): lax.psum_scatter(jnp.einsum('tf,df->td', active, dense_full[1], preferred...  67.4 us
    reduce_scatter x2, waiting for transfers between devices, shards(): lax.psum_scatter(jnp.einsum('tf,df->td', grad_hidden, dense_full[0], pref...  62.6 us
    ppermute x6, waiting for transfers between devices, shards(): lax.ppermute(ring[-1], 'mp', [(dev, (dev + 1) % 4) for dev in range(4)])  58.2 us
  transfers between devices with their start and end apart: 28, of which 27 were waited for; matrix products, arithmetic and copies ran while one was open for 8% of the time, Pallas kernels for 0%

profile of v1, /device:TPU:0, one launch (start us, length us, event | category | flops | bytes accessed | tf_op | source)
XLA Modules:
  0.0 1570.4 jit_solution(14997162840254335896)
XLA Ops:
  13.5 51.0 %all-gather.27.cloned.1.call-done = bf16[1,4,1024,256]{2,3,1,0:T(8,128)(2,1)} async-done(((bf16[1,4,128,256]{2,3,1,0:T(8,128)(2,1)}), bf16[1,4,1024,256]{2,3,1,0:T(8,128)(2,1)}) %all-gather.27.cloned.1.call-update) | async-done | bytes 2097168 | tf_op jit(solution)/shard_map/all_gather | solution.py:108
  64.4 25.9 %all-gather.15.cloned.1.call-done = bf16[1280,1024]{1,0:T(8,128)(2,1)} async-done(((bf16[320,1024]{1,0:T(8,128)(2,1)}), bf16[1280,1024]{1,0:T(8,128)(2,1)}) %all-gather.15.cloned.1.call-update) | async-done | bytes 2621456 | tf_op jit(solution)/shard_map/all_gather | solution.py:118
  94.8 11.0 fusion.135
  105.9 10.6 fusion.2
  116.5 11.0 fusion.57
  133.2 33.5 %reduce-scatter.13.cloned.1.call-done = bf16[320,1024]{1,0:T(8,128)(2,1)} async-done(((bf16[1280,1024]{1,0:T(8,128)(2,1)}), bf16[320,1024]{1,0:T(8,128)(2,1)}) %reduce-scatter.13.cloned.1.call-update) | async-done | bytes 655376 | tf_op jit(solution)/shard_map/reduce_scatter | solution.py:127
  169.4 10.0 collective-permute-done
  179.4 10.0 collective-permute-done.1
  189.9 10.1 collective-permute-done.2
  200.0 16.8 %fusion.36 = bf16[1280,1024]{1,0:T(8,128)(2,1)} fusion(s32[]{:T(128)S(6)} %select_n.24, bf16[320,1024]{1,0:T(8,128)(2,1)} %collective-permute-done.2, bf16[320,1024]{1,0:T(8,128)(2,1)S(1)} %collective-permute-done.1, bf16[320,1024]{1,0:T(8,128)(2,1)S(1)} %collective-permute-done, bf16[320,1024]{1,0:T(8,128)(2,1)S(1)} %add_convert_fusion.4), kind=kLoop, calls=%fused_computation.103 | loop fusion | flops 20971520 | bytes 5242884 | tf_op jit(solution)/shard_map/jit(_roll_dynamic)/concatenate | solution.py:140
  216.8 26.1 %all-gather.29.cloned.1.call-done = bf16[1,2,1024,1024]{3,2,1,0:T(8,128)(2,1)} async-done(((bf16[1,2,128,1024]{3,2,1,0:T(8,128)(2,1)}), bf16[1,2,1024,1024]{3,2,1,0:T(8,128)(2,1)}) %all-gather.29.cloned.1.call-update) | async-done | bytes 4194320 | tf_op jit(solution)/shard_map/all_gather | solution.py:109
  243.0 17.3 %multiply_convert_fusion.3 = (bf16[1280,1024]{1,0:T(8,128)(2,1)S(1)}, f32[1280,1024]{1,0:T(8,128)}, f32[1280,1024]{1,0:T(8,128)}) fusion(bf16[1280,1024]{1,0:T(8,128)(2,1)} %fusion.36, bf16[1,2,1024,1024]{3,2,1,0:T(8,128)(2,1)} %all-gather.29.cloned.1.call-done), kind=kOutput, calls=%fused_computation.63 | convolution fusion | flops 2769551360 | bytes 17825792 | tf_op jit(solution)/shard_map/dot_general | solution.py:145
  266.8 32.5 %reduce-scatter.15.cloned.1.call-done = bf16[320,1024]{1,0:T(8,128)(2,1)} async-done(((bf16[1280,1024]{1,0:T(8,128)(2,1)}), bf16[320,1024]{1,0:T(8,128)(2,1)}) %reduce-scatter.15.cloned.1.call-update) | async-done | bytes 655376 | tf_op jit(solution)/shard_map/reduce_scatter | solution.py:147
  302.1 50.7 %all-gather.31.cloned.1.call-done = bf16[1,4,1024,256]{2,3,1,0:T(8,128)(2,1)} async-done(((bf16[1,4,128,256]{2,3,1,0:T(8,128)(2,1)}), bf16[1,4,1024,256]{2,3,1,0:T(8,128)(2,1)}) %all-gather.31.cloned.1.call-update) | async-done | bytes 2097168 | tf_op jit(solution)/shard_map/all_gather | solution.py:108
  352.9 25.9 %all-gather.17.cloned.1.call-done = bf16[1280,1024]{1,0:T(8,128)(2,1)} async-done(((bf16[320,1024]{1,0:T(8,128)(2,1)}), bf16[1280,1024]{1,0:T(8,128)(2,1)}) %all-gather.17.cloned.1.call-update) | async-done | bytes 2621456 | tf_op jit(solution)/shard_map/all_gather | solution.py:118
  383.2 11.0 fusion.136
  394.2 10.6 fusion.3
  404.8 11.0 fusion.56
  420.9 34.0 %reduce-scatter.17.cloned.1.call-done = bf16[320,1024]{1,0:T(8,128)(2,1)} async-done(((bf16[1280,1024]{1,0:T(8,128)(2,1)}), bf16[320,1024]{1,0:T(8,128)(2,1)}) %reduce-scatter.17.cloned.1.call-update) | async-done | bytes 655376 | tf_op jit(solution)/shard_map/reduce_scatter | solution.py:127
  456.9 10.0 collective-permute-done.3
  467.7 10.1 collective-permute-done.4
  480.2 8.0 collective-permute-done.5
  488.2 13.2 fusion.29
  501.4 30.0 %all-gather.33.cloned.1.call-done = bf16[1,2,1024,1024]{3,2,1,0:T(8,128)(2,1)} async-done(((bf16[1,2,128,1024]{3,2,1,0:T(8,128)(2,1)}), bf16[1,2,1024,1024]{3,2,1,0:T(8,128)(2,1)}) %all-gather.33.cloned.1.call-update) | async-done | bytes 4194320 | tf_op jit(solution)/shard_map/all_gather | solution.py:109
  531.3 17.7 %multiply_convert_fusion.2 = (bf16[1280,1024]{1,0:T(8,128)(2,1)}, f32[1280,1024]{1,0:T(8,128)}, f32[1280,1024]{1,0:T(8,128)}) fusion(bf16[1280,1024]{1,0:T(8,128)(2,1)} %fusion.29, bf16[1,2,1024,1024]{3,2,1,0:T(8,128)(2,1)} %all-gather.33.cloned.1.call-done), kind=kOutput, calls=%fused_computation.50 | convolution fusion | flops 2769551360 | bytes 17825792 | tf_op jit(solution)/shard_map/dot_general | solution.py:145
  549.0 8.2 all-gather.19.cloned.1.call-done
  557.3 9.8 add_convert_fusion.1
  579.9 27.9 %reduce-scatter.21.cloned.1.call-done = bf16[320,1024]{1,0:T(8,128)(2,1)} async-done(((bf16[1280,1024]{1,0:T(8,128)(2,1)}), bf16[320,1024]{1,0:T(8,128)(2,1)}) %reduce-scatter.21.cloned.1.call-update) | async-done | bytes 655376 | tf_op jit(solution)/shard_map/reduce_scatter | solution.py:198
  609.9 34.9 %reduce-scatter.19.cloned.1.call-done = bf16[320,1024]{1,0:T(8,128)(2,1)} async-done(((bf16[1280,1024]{1,0:T(8,128)(2,1)}), bf16[320,1024]{1,0:T(8,128)(2,1)}) %reduce-scatter.19.cloned.1.call-update) | async-done | bytes 655376 | tf_op jit(solution)/shard_map/reduce_scatter | solution.py:147
  650.0 25.6 %all-gather.21.cloned.1.call-done = bf16[1280,1024]{1,0:T(8,128)(2,1)} async-done(((bf16[320,1024]{1,0:T(8,128)(2,1)}), bf16[1280,1024]{1,0:T(8,128)(2,1)}) %all-gather.21.cloned.1.call-update) | async-done | bytes 2621456 | tf_op jit(solution)/shard_map/all_gather | solution.py:209
  678.3 10.9 fusion.46
  689.2 16.7 %multiply_reduce_fusion.1 = (f32[4,1280]{1,0:T(4,128)S(1)}, f32[4,1280,1280]{1,2,0:T(8,128)}) fusion(f32[4,1280,1280]{1,2,0:T(8,128)} %get-tuple-element.130, f32[4,1280]{1,0:T(4,128)S(1)} %log_add_fusion.1, bf16[1280,4,64]{0,2,1:T(8,128)(2,1)S(1)} %bitcast.336, bf16[1280,3,4,64]{0,3,2,1:T(8,128)(2,1)} %bitcast.346), kind=kOutput, calls=%fused_computation.8 | convolution fusion | flops 858516480 | bytes 53780480 | tf_op jit(solution)/shard_map/qhe,khe->hqk/dot_general | solution.py:61
  705.9 22.2 %multiply_convert_fusion.1 = bf16[4,1280,1280]{1,2,0:T(8,128)(2,1)} fusion(f32[4,1280,1280]{1,2,0:T(8,128)} %get-tuple-element.133, f32[4,1280,1280]{1,2,0:T(8,128)} %get-tuple-element.130, f32[4,1280]{1,0:T(4,128)S(1)} %get-tuple-element.132, f32[4,1280]{1,0:T(4,128)S(1)} %log_add_fusion.1), kind=kLoop, calls=%fused_computation.7 | loop fusion | flops 26214400 | bytes 65576960 | tf_op jit(solution)/shard_map/convert_element_type | solution.py:65
  728.1 8.8 fusion.53
  752.3 34.5 %reduce-scatter.23.cloned.1.call-done = bf16[320,1024]{1,0:T(8,128)(2,1)} async-done(((bf16[1280,1024]{1,0:T(8,128)(2,1)}), bf16[320,1024]{1,0:T(8,128)(2,1)}) %reduce-scatter.23.cloned.1.call-update) | async-done | bytes 655376 | tf_op jit(solution)/shard_map/reduce_scatter | solution.py:229
  792.2 25.7 %all-gather.23.cloned.1.call-done = bf16[1280,1024]{1,0:T(8,128)(2,1)} async-done(((bf16[320,1024]{1,0:T(8,128)(2,1)}), bf16[1280,1024]{1,0:T(8,128)(2,1)}) %all-gather.23.cloned.1.call-update) | async-done | bytes 2621456 | tf_op jit(solution)/shard_map/all_gather | solution.py:190
  817.9 9.8 add_convert_fusion
  833.6 34.8 %reduce-scatter.25.cloned.1.call-done = bf16[320,1024]{1,0:T(8,128)(2,1)} async-done(((bf16[1280,1024]{1,0:T(8,128)(2,1)}), bf16[320,1024]{1,0:T(8,128)(2,1)}) %reduce-scatter.25.cloned.1.call-update) | async-done | bytes 655376 | tf_op jit(solution)/shard_map/reduce_scatter | solution.py:198
  874.3 25.2 %all-gather.25.cloned.1.call-done = bf16[1280,1024]{1,0:T(8,128)(2,1)} async-done(((bf16[320,1024]{1,0:T(8,128)(2,1)}), bf16[1280,1024]{1,0:T(8,128)(2,1)}) %all-gather.25.cloned.1.call-update) | async-done | bytes 2621456 | tf_op jit(solution)/shard_map/all_gather | solution.py:209
  902.3 11.7 fusion.49
  914.0 16.6 %multiply_reduce_fusion = (f32[4,1280]{1,0:T(4,128)S(1)}, f32[4,1280,1280]{1,2,0:T(8,128)}) fusion(f32[4,1280,1280]{1,2,0:T(8,128)} %get-tuple-element.127, f32[4,1280]{1,0:T(4,128)S(1)} %log_add_fusion, bf16[1280,4,64]{0,2,1:T(8,128)(2,1)S(1)} %bitcast.338, bf16[1280,3,4,64]{0,3,2,1:T(8,128)(2,1)S(1)} %bitcast.341), kind=kOutput, calls=%fused_computation.5 | convolution fusion | flops 858516480 | bytes 53780480 | tf_op jit(solution)/shard_map/qhe,khe->hqk/dot_general | solution.py:61
  930.5 22.0 %multiply_convert_fusion = bf16[4,1280,1280]{1,2,0:T(8,128)(2,1)} fusion(f32[4,1280,1280]{1,2,0:T(8,128)} %get-tuple-element.135, f32[4,1280,1280]{1,2,0:T(8,128)} %get-tuple-element.127, f32[4,1280]{1,0:T(4,128)S(1)} %get-tuple-element.134, f32[4,1280]{1,0:T(4,128)S(1)} %log_add_fusion), kind=kLoop, calls=%fused_computation.4 | loop fusion | flops 26214400 | bytes 65576960 | tf_op jit(solution)/shard_map/convert_element_type | solution.py:65
  952.6 8.8 fusion.55
  1034.5 129.0 %reduce-scatter.35.cloned.1.call-done = f32[2,128,1024]{2,1,0:T(8,128)} async-done(((f32[2,1024,1024]{2,1,0:T(8,128)}), f32[2,128,1024]{2,1,0:T(8,128)}) %reduce-scatter.35.cloned.1.call-update) | async-done | bytes 1048592 | tf_op jit(solution)/shard_map/reduce_scatter | solution.py:244
  1163.5 151.9 %reduce-scatter.31.cloned.1.call-done = f32[2,128,1024]{2,1,0:T(8,128)} async-done(((f32[2,1024,1024]{2,1,0:T(8,128)}), f32[2,128,1024]{2,1,0:T(8,128)}) %reduce-scatter.31.cloned.1.call-update) | async-done | bytes 1048592 | tf_op jit(solution)/shard_map/reduce_scatter | solution.py:244
  1323.5 83.2 %reduce-scatter.33.cloned.1.call-done = f32[4,128,256]{1,2,0:T(8,128)} async-done(((f32[4,1024,256]{1,2,0:T(8,128)}), f32[4,128,256]{1,2,0:T(8,128)}) %reduce-scatter.33.cloned.1.call-update) | async-done | bytes 524304 | tf_op jit(solution)/shard_map/reduce_scatter | solution.py:243
  1406.6 92.3 %reduce-scatter.29.cloned.1.call-done = f32[4,128,256]{1,2,0:T(8,128)} async-done(((f32[4,1024,256]{1,2,0:T(8,128)}), f32[4,128,256]{1,2,0:T(8,128)}) %reduce-scatter.29.cloned.1.call-update) | async-done | bytes 524304 | tf_op jit(solution)/shard_map/reduce_scatter | solution.py:243
  1503.4 40.8 %all-reduce = (f32[1,6,2]{1,2,0:T(2,128)S(1)}, f32[1,6,2]{1,2,0:T(2,128)S(1)}, f32[1,4,1024]{2,1,0:T(4,128)S(1)}, f32[1,4,1024]{2,1,0:T(4,128)S(1)}) all-reduce(f32[1,6,2]{1,2,0:T(2,128)S(1)} %maximum_bitcast_fusion.2, f32[1,6,2]{1,2,0:T(2,128)S(1)} %maximum_bitcast_fusion.3, ...), channel_id=1, replica_groups=mesh['dp'=8,'mp'=4] {'dp','mp'}, use_global_device_ids=true, to_apply=%region_36.38 | all-reduce | flops 8216 | bytes 65728 | tf_op jit(solution)/shard_map/psum | solution.py:286
  (347 shorter events, 205.2 us)
Async XLA Ops:
  7.2 57.3 %all-gather.27.cloned.1.call-start = ((), (), s32[]{:S(2)}) async-start(), calls=%async_computation.30 | async-start | bytes 2359296 | tf_op jit(solution)/shard_map/all_gather | solution.py:108
  10.0 80.3 %all-gather.15.cloned.1.call-start = ((), (), s32[]{:S(2)}) async-start(), calls=%async_computation.12 | async-start | bytes 3276800 | tf_op jit(solution)/shard_map/all_gather | solution.py:118
  10.6 84.2 %copy-start.64 = (f32[320]{0:T(512)}, f32[320]{0:T(512)S(1)}, u32[]{:S(2)}) copy-start(f32[320]{0:T(512)S(1)} %fusion.107) | copy-start | bytes 3844
  11.2 157.2 %copy-start.54 = (f32[1,1,1024]{2,1,0:T(1,128)}, f32[1,1,1024]{2,1,0:T(1,128)S(1)}, u32[]{:S(2)}) copy-start(f32[1,1,1024]{2,1,0:T(1,128)S(1)} %get-tuple-element.116) | copy-start | bytes 12292
  11.2 289.7 %copy-start.44 = (f32[1,1,1024]{2,1,0:T(1,128)}, f32[1,1,1024]{2,1,0:T(1,128)S(1)}, u32[]{:S(2)}) copy-start(f32[1,1,1024]{2,1,0:T(1,128)S(1)} %get-tuple-element.114) | copy-start | bytes 12292
  12.4 154.3 %reduce-scatter.13.cloned.1.call-start = ((), (), s32[]{:S(2)}) async-start(), calls=%async_computation.13 | async-start | bytes 3276800 | tf_op jit(solution)/shard_map/reduce_scatter | solution.py:127
  13.4 81.4 %copy-start.22 = (pred[1280,1280]{0,1:T(8,128)(4,1)}, pred[1280,1280]{0,1:T(8,128)(4,1)S(1)}, u32[]{:S(2)}) copy-start(pred[1280,1280]{0,1:T(8,128)(4,1)S(1)} %broadcast_compare_fusion) | copy-start | bytes 4915204
  131.9 111.1 %all-gather.29.cloned.1.call-start = ((), (), s32[]{:S(2)}) async-start(), calls=%async_computation.31 | async-start | bytes 4718592 | tf_op jit(solution)/shard_map/all_gather | solution.py:109
  133.2 166.1 %reduce-scatter.15.cloned.1.call-start = ((), (), s32[]{:S(2)}) async-start(), calls=%async_computation.14 | async-start | bytes 3276800 | tf_op jit(solution)/shard_map/reduce_scatter | solution.py:147
  168.0 131.2 %copy-start.2 = (f32[320,1024]{1,0:T(8,128)}, f32[320,1024]{1,0:T(8,128)S(1)}, u32[]{:S(2)}) copy-start(f32[320,1024]{1,0:T(8,128)S(1)} %get-tuple-element.80) | copy-start | bytes 3932164
  169.4 10.1 collective-permute-start
  179.4 10.0 collective-permute-start.1
  189.4 10.6 collective-permute-start.2
  266.2 86.7 %all-gather.31.cloned.1.call-start = ((), (), s32[]{:S(2)}) async-start(), calls=%async_computation.32 | async-start | bytes 2359296 | tf_op jit(solution)/shard_map/all_gather | solution.py:108
  266.7 112.0 %all-gather.17.cloned.1.call-start = ((), (), s32[]{:S(2)}) async-start(), calls=%async_computation.15 | async-start | bytes 3276800 | tf_op jit(solution)/shard_map/all_gather | solution.py:118
  302.1 81.1 %copy-start.23 = (pred[1280,1280]{0,1:T(8,128)(4,1)S(1)}, pred[1280,1280]{0,1:T(8,128)(4,1)}, u32[]{:S(2)}) copy-start(pred[1280,1280]{0,1:T(8,128)(4,1)} %copy-done.22) | copy-start | bytes 4915204
  302.1 152.8 %reduce-scatter.17.cloned.1.call-start = ((), (), s32[]{:S(2)}) async-start(), calls=%async_computation.16 | async-start | bytes 3276800 | tf_op jit(solution)/shard_map/reduce_scatter | solution.py:127
  420.1 36.5 %copy-start.56 = (f32[1,1,1024]{2,1,0:T(1,128)S(1)}, f32[1,1,1024]{2,1,0:T(1,128)}, u32[]{:S(2)}) copy-start(f32[1,1,1024]{2,1,0:T(1,128)} %get-tuple-element.111) | copy-start | bytes 12292
  420.1 36.5 %copy-start.76 = (f32[1,1,1024]{2,1,0:T(1,128)S(1)}, f32[1,1,1024]{2,1,0:T(1,128)}, u32[]{:S(2)}) copy-start(f32[1,1,1024]{2,1,0:T(1,128)} %get-tuple-element.112) | copy-start | bytes 12292
  420.1 111.2 %all-gather.33.cloned.1.call-start = ((), (), s32[]{:S(2)}) async-start(), calls=%async_computation.33 | async-start | bytes 4718592 | tf_op jit(solution)/shard_map/all_gather | solution.py:109
  420.8 136.4 %all-gather.19.cloned.1.call-start = ((), (), s32[]{:S(2)}) async-start(), calls=%async_computation.18 | async-start | bytes 3276800 | tf_op jit(solution)/shard_map/all_gather | solution.py:190
  456.8 10.1 collective-permute-start.3
  467.7 10.1 collective-permute-start.4
  477.9 10.3 collective-permute-start.5
  480.2 127.6 %reduce-scatter.21.cloned.1.call-start = ((), (), s32[]{:S(2)}) async-start(), calls=%async_computation.19 | async-start | bytes 3276800 | tf_op jit(solution)/shard_map/reduce_scatter | solution.py:198
  572.9 71.9 %reduce-scatter.19.cloned.1.call-start = ((), (), s32[]{:S(2)}) async-start(), calls=%async_computation.17 | async-start | bytes 3276800 | tf_op jit(solution)/shard_map/reduce_scatter | solution.py:147
  579.8 95.8 %all-gather.21.cloned.1.call-start = ((), (), s32[]{:S(2)}) async-start(), calls=%async_computation.20 | async-start | bytes 3276800 | tf_op jit(solution)/shard_map/all_gather | solution.py:209
  649.9 137.0 %reduce-scatter.23.cloned.1.call-start = ((), (), s32[]{:S(2)}) async-start(), calls=%async_computation.21 | async-start | bytes 3276800 | tf_op jit(solution)/shard_map/reduce_scatter | solution.py:229
  752.0 36.4 %copy-start.73 = (f32[320]{0:T(512)S(1)}, f32[320]{0:T(512)}, u32[]{:S(2)}) copy-start(f32[320]{0:T(512)} %copy-done.72) | copy-start | bytes 3844
  752.0 36.5 %copy-start.67 = (f32[320]{0:T(512)S(1)}, f32[320]{0:T(512)}, u32[]{:S(2)}) copy-start(f32[320]{0:T(512)} %copy-done.66) | copy-start | bytes 3844
  752.0 38.2 %copy-start.10 = (f32[320,1024]{1,0:T(8,128)S(1)}, f32[320,1024]{1,0:T(8,128)}, u32[]{:S(2)}) copy-start(f32[320,1024]{1,0:T(8,128)} %param.16) | copy-start | bytes 3932164
  752.0 65.9 %all-gather.23.cloned.1.call-start = ((), (), s32[]{:S(2)}) async-start(), calls=%async_computation.22 | async-start | bytes 3276800 | tf_op jit(solution)/shard_map/all_gather | solution.py:190
  792.2 76.2 %reduce-scatter.25.cloned.1.call-start = ((), (), s32[]{:S(2)}) async-start(), calls=%async_computation.23 | async-start | bytes 3276800 | tf_op jit(solution)/shard_map/reduce_scatter | solution.py:198
  833.5 34.9 %copy-start.3 = (f32[320,1024]{1,0:T(8,128)S(1)}, f32[320,1024]{1,0:T(8,128)}, u32[]{:S(2)}) copy-start(f32[320,1024]{1,0:T(8,128)} %copy-done.2) | copy-start | bytes 3932164
  833.5 34.9 %copy-start.55 = (f32[1,1,1024]{2,1,0:T(1,128)S(1)}, f32[1,1,1024]{2,1,0:T(1,128)}, u32[]{:S(2)}) copy-start(f32[1,1,1024]{2,1,0:T(1,128)} %copy-done.54) | copy-start | bytes 12292
  833.5 34.9 %copy-start.58 = (f32[320]{0:T(512)S(1)}, f32[320]{0:T(512)}, u32[]{:S(2)}) copy-start(f32[320]{0:T(512)} %copy-done.57) | copy-start | bytes 3844
  833.5 34.9 %copy-start.63 = (f32[320]{0:T(512)S(1)}, f32[320]{0:T(512)}, u32[]{:S(2)}) copy-start(f32[320]{0:T(512)} %copy-done.62) | copy-start | bytes 3844
  833.5 36.5 %copy-start.71 = (f32[320]{0:T(512)S(1)}, f32[320]{0:T(512)}, u32[]{:S(2)}) copy-start(f32[320]{0:T(512)} %copy-done.70) | copy-start | bytes 3844
  833.5 39.1 %copy-start.11 = (f32[320,1024]{1,0:T(8,128)S(1)}, f32[320,1024]{1,0:T(8,128)}, u32[]{:S(2)}) copy-start(f32[320,1024]{1,0:T(8,128)} %get-tuple-element.68) | copy-start | bytes 3932164
  833.6 66.0 %all-gather.25.cloned.1.call-start = ((), (), s32[]{:S(2)}) async-start(), calls=%async_computation.24 | async-start | bytes 3276800 | tf_op jit(solution)/shard_map/all_gather | solution.py:209
  873.8 153.8 %reduce-scatter.27.cloned.1.call-start = ((), (), s32[]{:S(2)}) async-start(), calls=%async_computation.25 | async-start | bytes 3276800 | tf_op jit(solution)/shard_map/reduce_scatter | solution.py:229
  976.0 187.5 %reduce-scatter.35.cloned.1.call-start = ((), (), s32[]{:S(2)}) async-start(), calls=%async_computation.29 | async-start | bytes 9437184 | tf_op jit(solution)/shard_map/reduce_scatter | solution.py:244
  989.9 325.6 %reduce-scatter.31.cloned.1.call-start = ((), (), s32[]{:S(2)}) async-start(), calls=%async_computation.27 | async-start | bytes 9437184 | tf_op jit(solution)/shard_map/reduce_scatter | solution.py:244
  1003.7 403.0 %reduce-scatter.33.cloned.1.call-start = ((), (), s32[]{:S(2)}) async-start(), calls=%async_computation.28 | async-start | bytes 4718592 | tf_op jit(solution)/shard_map/reduce_scatter | solution.py:243
  1013.7 485.3 %reduce-scatter.29.cloned.1.call-start = ((), (), s32[]{:S(2)}) async-start(), calls=%async_computation.26 | async-start | bytes 4718592 | tf_op jit(solution)/shard_map/reduce_scatter | solution.py:243
  1031.0 284.5 %copy-start.5 = (f32[2,2,128,1024]{3,2,1,0:T(8,128)S(1)}, f32[2,2,128,1024]{3,2,1,0:T(8,128)}, u32[]{:S(2)}) copy-start(f32[2,2,128,1024]{3,2,1,0:T(8,128)} %param.21) | copy-start | bytes 6291460
  1321.1 177.8 %copy-start.7 = (f32[2,4,128,256]{2,3,1,0:T(8,128)S(1)}, f32[2,4,128,256]{2,3,1,0:T(8,128)}, u32[]{:S(2)}) copy-start(f32[2,4,128,256]{2,3,1,0:T(8,128)} %copy-done.6) | copy-start | bytes 3145732
  1323.5 220.7 %copy-start.77 = (f32[6]{0:T(128)S(1)}, f32[6]{0:T(128)}, u32[]{:S(2)}) copy-start(f32[6]{0:T(128)} %constant.161) | copy-start | bytes 76
  (69 other events, 358.8 us)
Sparse Core Ops, SparseCore 0:
  10.6 53.7 all-gather.26
  66.6 23.7 all-gather.14
  132.0 34.6 reduce-scatter.12
  169.6 73.3 all-gather.28
  266.3 32.9 reduce-scatter.14
  301.7 51.0 all-gather.30
  355.0 23.7 all-gather.16
  420.2 34.6 reduce-scatter.16
  457.9 73.3 all-gather.32
  533.4 23.8 all-gather.18
  573.0 34.6 reduce-scatter.20
  610.1 34.6 reduce-scatter.18
  650.0 25.5 all-gather.20
  752.1 34.6 reduce-scatter.22
  792.3 25.5 all-gather.22
  833.7 34.6 reduce-scatter.24
  873.9 25.5 all-gather.24
  976.2 34.6 reduce-scatter.26
  1014.5 149.0 reduce-scatter.34
  1167.5 147.9 reduce-scatter.30
  1319.1 87.4 reduce-scatter.32
  1410.7 88.1 reduce-scatter.28
